TPU v7x, 32 devices: a whole 2x2x4 slice. The times are simulated.
32 devices in a mesh: ex: 8 (over z, y), par: 4 (over x, core).
Axes of the slice: x: 2, y: 2, z: 4, core: 2. Of those that a mesh axis runs over, the one named last changes fastest.
Arguments:
- gradients: bfloat16 [512, 16384], P('ex', 'par'), may hold values from -6 to 6
- inverse_gram: bfloat16 [16384, 16384], P('par', 'ex'), may hold values from -1 to 3
- hash_words: int32 [4], replicated, may hold values from 1 to 2147483646
Outputs:
- scores: float32 [512, 512], P('par', 'ex')
All inputs are finite; a program needn't handle non-finite values.
Results may differ from a plain program's by a relative error of at most 0.0003.
Values may be sent and summed in bfloat16 or wider, within the bound.
A program may use at most 64 MiB of HBM per device.

v0:
```python
import math

import jax
import jax.numpy as jnp
from jax import lax
from jax.sharding import PartitionSpec as P

FEATURES = 16384


def shifted(values, amount):
    return lax.shift_right_logical(values, jnp.full(values.shape, amount, jnp.int32))


def hash_table(hash_words, row_start, row_count, col_start, col_count):
    row_ids = lax.broadcasted_iota(jnp.int32, (row_count, col_count), 0) + row_start
    col_ids = lax.broadcasted_iota(jnp.int32, (row_count, col_count), 1) + col_start
    mixed = row_ids * FEATURES + col_ids
    mixed = mixed * (hash_words[0] | 1) + hash_words[1]
    mixed = mixed ^ shifted(mixed, 15)
    mixed = mixed * (hash_words[2] | 1)
    mixed = mixed ^ shifted(mixed, 13)
    mixed = mixed * (hash_words[3] | 1)
    mixed = mixed ^ shifted(mixed, 16)
    top_bit = shifted(mixed, 31)
    return ((1 - 2 * top_bit).astype(jnp.float32) * FEATURES ** (-0.5)).astype(jnp.bfloat16)


def per_device(gradients, inverse_gram, hash_words):
    ex_rows, param_width = gradients.shape
    feat_par = inverse_gram.shape[0]
    par_index = lax.axis_index("par")
    zeroed = jnp.zeros((ex_rows, feat_par), jnp.float32)
    portion = lax.all_gather(gradients, "par", axis=1, tiled=True)
    amount = portion.shape[1]
    stride = math.gcd(amount, 4096)

    def row_turn(turn_index, partial_sum):
        row_part = lax.dynamic_slice_in_dim(portion, turn_index * stride, stride, 1)
        sign_table = hash_table(
            hash_words, turn_index * stride, stride, par_index * feat_par, feat_par
        )
        return partial_sum + jnp.dot(row_part, sign_table, preferred_element_type=jnp.float32)

    projected = lax.fori_loop(0, amount // stride, row_turn, zeroed)
    features = projected.astype(jnp.bfloat16)
    partials = jnp.dot(
        lax.all_gather(features, "ex", axis=0, tiled=True),
        inverse_gram,
        preferred_element_type=jnp.float32,
    )
    conditioned = lax.psum_scatter(partials, "par", scatter_dimension=0, tiled=True).astype(
        jnp.bfloat16
    )
    feature_rows = lax.all_gather(features, "par", axis=1, tiled=True)
    pairs = lax.dot_general(
        lax.all_gather(conditioned, "ex", axis=1, tiled=True),
        feature_rows,
        (((1,), (1,)), ((), ())),
        preferred_element_type=jnp.float32,
    )
    return pairs * FEATURES ** (-0.5)


def solution(mesh):
    return jax.shard_map(
        per_device,
        mesh=mesh,
        in_specs=(P("ex", "par"), P("par", "ex"), P()),
        out_specs=P("par", "ex"),
        check_vma=False,
    )
```

profile of v0, /device:TPU:0, one launch (start us, length us, event | category | flops | bytes accessed | tf_op | source)
XLA Modules:
  0.0 440.9 jit_solution(11616571653855265152)
XLA Ops:
  6.5 0.0 all-gather.5.cloned.1.call-start
  6.5 0.7 all-gather.5.cloned.1.call-update
  7.3 0.0 all-gather.7.cloned.1.call-start
  7.3 1.4 fusion.22
  10.6 23.6 %all-gather.5.cloned.1.call-done = bf16[64,16384]{1,0:T(8,128)(2,1)} async-done(((bf16[64,4096]{1,0:T(8,128)(2,1)}), bf16[64,16384]{1,0:T(8,128)(2,1)}) %all-gather.5.cloned.1.call-update) | async-done | bytes 2097168 | tf_op jit(solution)/shard_map/all_gather | solution.py:34
  34.2 164.2 %while.16 = (s32[]{:T(128)}, f32[64,4096]{1,0:T(8,128)S(1)}, bf16[64,16384]{1,0:T(8,128)(2,1)}, s32[]{:T(128)}, s32[]{:T(128)}, /*index=5*/s32[4]{0:T(128)}, s32...) while((s32[]{:T(128)}, f32[64,4096]{1,0:T(8,128)S(1)}, ...), condition=%wide.region_1.0_spmd.clone, body=%wide.region_0.0_spmd.clone.sunk | while | flops 2433232896 | bytes 2689225 | solution.py:45
  34.2 1.3 slice.44
  35.5 39.7 %fusion.33 = f32[64,4096]{1,0:T(8,128)S(1)} fusion(s32[]{:T(128)} %get-tuple-element.282, s32[]{:T(128)} %get-tuple-element.281, s32[]{:T(128)} %bitcast.9, s32[]{:T(128)} %get-tuple-element.279, s32[4096]{0:T(1024)S(1)} %get-tuple-element.249, s32[4096]{0:T(1024)S(1)} %get-tuple-element.250, f32[64,4096]{1,0:T(8,128)S(1)} %get-tuple-element.264, ...), kind=kOutput, calls=%fused_computation.12.clone.1 | convolution fusion | flops 2433220608 | bytes 2656261 | tf_op jit(solution)/shard_map/while/body/eval_jaxpr/dot_general | solution.py:43
  75.3 1.3 slice.44
  76.6 39.7 %fusion.33 = f32[64,4096]{1,0:T(8,128)S(1)} fusion(s32[]{:T(128)} %get-tuple-element.282, s32[]{:T(128)} %get-tuple-element.281, s32[]{:T(128)} %bitcast.9, s32[]{:T(128)} %get-tuple-element.279, s32[4096]{0:T(1024)S(1)} %get-tuple-element.249, s32[4096]{0:T(1024)S(1)} %get-tuple-element.250, f32[64,4096]{1,0:T(8,128)S(1)} %get-tuple-element.264, ...), kind=kOutput, calls=%fused_computation.12.clone.1 | convolution fusion | flops 2433220608 | bytes 2656261 | tf_op jit(solution)/shard_map/while/body/eval_jaxpr/dot_general | solution.py:43
  116.3 1.3 slice.44
  117.6 39.7 %fusion.33 = f32[64,4096]{1,0:T(8,128)S(1)} fusion(s32[]{:T(128)} %get-tuple-element.282, s32[]{:T(128)} %get-tuple-element.281, s32[]{:T(128)} %bitcast.9, s32[]{:T(128)} %get-tuple-element.279, s32[4096]{0:T(1024)S(1)} %get-tuple-element.249, s32[4096]{0:T(1024)S(1)} %get-tuple-element.250, f32[64,4096]{1,0:T(8,128)S(1)} %get-tuple-element.264, ...), kind=kOutput, calls=%fused_computation.12.clone.1 | convolution fusion | flops 2433220608 | bytes 2656261 | tf_op jit(solution)/shard_map/while/body/eval_jaxpr/dot_general | solution.py:43
  157.4 1.3 slice.44
  158.7 39.7 %fusion.33 = f32[64,4096]{1,0:T(8,128)S(1)} fusion(s32[]{:T(128)} %get-tuple-element.282, s32[]{:T(128)} %get-tuple-element.281, s32[]{:T(128)} %bitcast.9, s32[]{:T(128)} %get-tuple-element.279, s32[4096]{0:T(1024)S(1)} %get-tuple-element.249, s32[4096]{0:T(1024)S(1)} %get-tuple-element.250, f32[64,4096]{1,0:T(8,128)S(1)} %get-tuple-element.264, ...), kind=kOutput, calls=%fused_computation.12.clone.1 | convolution fusion | flops 2433220608 | bytes 2656261 | tf_op jit(solution)/shard_map/while/body/eval_jaxpr/dot_general | solution.py:43
  198.4 0.9 convert_element_type.24
  199.3 0.0 all-gather.7.cloned.1.call-update
  199.4 0.2 reduce-scatter.2.cloned.1.call-start
  199.6 72.7 %all-gather.7.cloned.1.call-done = bf16[512,4096]{1,0:T(8,128)(2,1)} async-done(((bf16[64,4096]{1,0:T(8,128)(2,1)}), bf16[512,4096]{1,0:T(8,128)(2,1)}) %all-gather.7.cloned.1.call-update) | async-done | bytes 4194320 | tf_op jit(solution)/shard_map/all_gather | solution.py:48
  272.3 14.9 %fusion.23 = f32[512,2048]{1,0:T(8,128)} fusion(bf16[512,4096]{1,0:T(8,128)(2,1)} %all-gather.7.cloned.1.call-done, bf16[4096,2048]{1,0:T(8,128)(2,1)} %param.6), kind=kOutput, calls=%fused_computation.26 | convolution fusion | flops 8589934592 | bytes 25165824 | tf_op jit(solution)/shard_map/dot_general | solution.py:47
  287.2 0.0 reduce-scatter.2.cloned.1.call-update
  287.2 0.0 all-gather.11.cloned.1.call-start
  287.3 0.5 all-gather.11.cloned.1.call-update
  287.8 0.0 all-gather.9.cloned.1.call-start
  287.9 42.6 %reduce-scatter.2.cloned.1.call-done = f32[128,2048]{1,0:T(8,128)} async-done(((f32[512,2048]{1,0:T(8,128)}), f32[128,2048]{1,0:T(8,128)}) %reduce-scatter.2.cloned.1.call-update) | async-done | bytes 1048592 | tf_op jit(solution)/shard_map/reduce_scatter | solution.py:52
  330.5 2.1 convert_element_type.25
  332.6 0.0 all-gather.9.cloned.1.call-update
  332.6 21.9 %all-gather.11.cloned.1.call-done = bf16[64,16384]{1,0:T(8,128)(2,1)} async-done(((bf16[64,4096]{1,0:T(8,128)(2,1)}), bf16[64,16384]{1,0:T(8,128)(2,1)}) %all-gather.11.cloned.1.call-update) | async-done | bytes 2097168 | tf_op jit(solution)/shard_map/all_gather | solution.py:55
  354.5 74.8 %all-gather.9.cloned.1.call-done = bf16[128,16384]{1,0:T(8,128)(2,1)} async-done(((bf16[128,2048]{1,0:T(8,128)(2,1)}), bf16[128,16384]{1,0:T(8,128)(2,1)}) %all-gather.9.cloned.1.call-update) | async-done | bytes 4194320 | tf_op jit(solution)/shard_map/all_gather | solution.py:57
  429.4 5.1 %convolution_multiply_fusion = f32[128,64]{0,1:T(8,128)} fusion(bf16[128,16384]{1,0:T(8,128)(2,1)} %all-gather.9.cloned.1.call-done, bf16[64,16384]{1,0:T(8,128)(2,1)} %all-gather.11.cloned.1.call-done), kind=kOutput, calls=%fused_computation.24 | convolution fusion | flops 268443648 | bytes 6324224 | tf_op jit(solution)/shard_map/dot_general | solution.py:56
  (5 shorter events, 0.0 us)
Async XLA Ops:
  6.5 27.7 %all-gather.5.cloned.1.call-start = ((), (), s32[]{:S(2)}) async-start(), calls=%async_computation.1 | async-start | bytes 2621440 | tf_op jit(solution)/shard_map/all_gather | solution.py:34
  7.3 265.0 %all-gather.7.cloned.1.call-start = ((), (), s32[]{:S(2)}) async-start(), calls=%async_computation.2 | async-start | bytes 4718592 | tf_op jit(solution)/shard_map/all_gather | solution.py:48
  199.4 131.2 %reduce-scatter.2.cloned.1.call-start = ((), (), s32[]{:S(2)}) async-start(), calls=%async_computation.3 | async-start | bytes 5242880 | tf_op jit(solution)/shard_map/reduce_scatter | solution.py:52
  287.2 67.3 %all-gather.11.cloned.1.call-start = ((), (), s32[]{:S(2)}) async-start(), calls=%async_computation.5 | async-start | bytes 2621440 | tf_op jit(solution)/shard_map/all_gather | solution.py:55
  287.8 141.5 %all-gather.9.cloned.1.call-start = ((), (), s32[]{:S(2)}) async-start(), calls=%async_computation.4 | async-start | bytes 4718592 | tf_op jit(solution)/shard_map/all_gather | solution.py:57
Sparse Core Ops, SparseCore 0:
  8.9 25.2 all-gather.4
  199.5 72.7 all-gather.6
  287.4 43.1 reduce-scatter.1
  331.9 22.5 all-gather.10
  356.6 72.7 all-gather.8
where the time goes:
time: 441 us
  waiting for transfers between devices  237 us (54%)
  matrix products  179 us (41%)
  between operations  15 us (3%)
  local copies, waits for them, and re-layouts  6.66 us (2%)
    dot_general x4, matrix products, row_turn(): jnp.dot(row_part, sign_table, preferred_element_type=jnp.float32)  159 us
    all_gather x1, waiting for transfers between devices, per_device(): lax.all_gather(conditioned, 'ex', axis=1, tiled=True)  74.8 us
    all_gather x1, waiting for transfers between devices, per_device(): lax.all_gather(features, 'ex', axis=0, tiled=True)  72.7 us
    reduce_scatter x1, waiting for transfers between devices, per_device(): lax.psum_scatter(partials, 'par', scatter_dimension=0, tiled=True)  42.6 us
    all_gather x1, waiting for transfers between devices, per_device(): portion = lax.all_gather(gradients, 'par', axis=1, tiled=True)  23.6 us
    all_gather x1, waiting for transfers between devices, per_device(): feature_rows = lax.all_gather(features, 'par', axis=1, tiled=True)  21.9 us
    dot_general x1, matrix products, per_device(): jnp.dot(lax.all_gather(features, 'ex', axis=0, tiled=True), inverse_gram,...  14.9 us
  transfers between devices with their start and end apart: 5, of which 5 were waited for; matrix products, arithmetic and copies ran while one was open for 1% of the time, Pallas kernels for 0%

commit v1 on v0

v1 whole, which is shorter than its diff:
```python
import functools

import jax
import jax.numpy as jnp
from jax import lax
from jax.experimental import pallas as pl
from jax.experimental.pallas import tpu as pltpu
from jax.sharding import PartitionSpec as P

FEATURES = 16384


def shifted(values, amount):
    return lax.shift_right_logical(values, jnp.full(values.shape, amount, jnp.int32))


def hash_kernel(tile, words_ref, start_ref, cols_ref, grads_ref, out_ref):
    step = pl.program_id(0)
    depth = grads_ref.shape[1]
    m0 = words_ref[0] | 1
    m2 = words_ref[2] | 1
    m3 = words_ref[3] | 1
    row_base = (start_ref[0] + step * depth) * FEATURES * m0 + words_ref[1]
    rows = lax.broadcasted_iota(jnp.int32, (depth, tile), 0) * (m0 * FEATURES)
    grads = grads_ref[...]
    for first in range(0, out_ref.shape[1], tile):
        mixed = rows + (cols_ref[:, first:first + tile] * m0 + row_base)
        mixed = (mixed ^ shifted(mixed, 15)) * m2
        mixed = (mixed ^ shifted(mixed, 13)) * m3
        signs = jnp.where(mixed < 0, -1.0, 1.0).astype(jnp.bfloat16)
        part = jnp.dot(grads, signs, preferred_element_type=jnp.float32)

        @pl.when(step == 0)
        def _():
            out_ref[:, first:first + tile] = part

        @pl.when(step > 0)
        def _():
            out_ref[:, first:first + tile] += part


def project(words, start, cols, grads):
    rows, amount = grads.shape
    width = cols.shape[1]
    depth = min(512, amount)
    tile = min(512, width)
    return pl.pallas_call(
        functools.partial(hash_kernel, tile),
        grid=(amount // depth,),
        in_specs=[
            pl.BlockSpec(memory_space=pltpu.SMEM),
            pl.BlockSpec(memory_space=pltpu.SMEM),
            pl.BlockSpec((1, width), lambda k: (0, 0)),
            pl.BlockSpec((rows, depth), lambda k: (0, k)),
        ],
        out_specs=pl.BlockSpec((rows, width), lambda k: (0, 0)),
        out_shape=jax.ShapeDtypeStruct((rows, width), jnp.float32),
        compiler_params=pltpu.CompilerParams(
            dimension_semantics=("arbitrary",), vmem_limit_bytes=48 << 20
        ),
    )(words, start, cols, grads)


def per_device(ex_n, par_n, gradients, inverse_gram, hash_words):
    amount = gradients.shape[1]
    feat_par, feat_ex = inverse_gram.shape
    piece = feat_par // ex_n
    e, p = lax.axis_index("ex"), lax.axis_index("par")
    ids = jnp.arange(feat_ex, dtype=jnp.int32)
    cols = (ids // piece) * feat_par + e * piece + ids % piece
    everyone = lax.all_gather(gradients, "ex", axis=0, tiled=True)
    partial = project(hash_words, (p * amount)[None], cols[None, :], everyone)
    summed = lax.psum_scatter(partial, "par", scatter_dimension=1, tiled=True)
    mine = (summed * FEATURES ** (-0.5)).astype(jnp.bfloat16)
    feat_p = lax.all_gather(mine, "ex", axis=1, tiled=True)
    pairs = []
    for src_e in range(ex_n):
        for src_p in range(par_n):
            pairs.append((src_e * par_n + src_p, src_p * ex_n + src_e))
    moved = lax.ppermute(mine, ("ex", "par"), pairs)
    feat_e = lax.all_gather(moved, "par", axis=1, tiled=True)
    parts = jnp.dot(feat_p, inverse_gram, preferred_element_type=jnp.float32)
    conditioned = lax.psum_scatter(parts, "par", scatter_dimension=0, tiled=True)
    scores = lax.dot_general(
        conditioned.astype(jnp.bfloat16),
        feat_e,
        (((1,), (1,)), ((), ())),
        preferred_element_type=jnp.float32,
    )
    scores = lax.psum_scatter(scores, "ex", scatter_dimension=1, tiled=True)
    return scores * FEATURES ** (-0.5)


def solution(mesh):
    return jax.shard_map(
        functools.partial(per_device, mesh.shape["ex"], mesh.shape["par"]),
        mesh=mesh,
        in_specs=(P("ex", "par"), P("par", "ex"), P()),
        out_specs=P("par", "ex"),
        check_vma=False,
    )
```

time: 441 us -> 388 us (0.88)
  matrix products: 179 us -> 18.3 us
  waiting for transfers between devices: 237 us -> 324 us
  Pallas kernels: 0 us -> 24 us
    dot_general x6 -> x2, matrix products: 179 us -> 18.3 us  [the longest x1 14.9 us: per_device(): parts = jnp.dot(feat_p, inverse_gram, preferred_element_type=jnp.float32)]
    reduce_scatter x1 -> x3, waiting for transfers between devices: 42.6 us -> 152 us  [the longest x1 62.2 us: per_device(): scores = lax.psum_scatter(scores, 'ex', scatter_dimension=1, tiled=True)]
    pallas_call x0 -> x1, Pallas kernels: none -> 24 us  [project(): pl.pallas_call(functools.partial(hash_kernel, tile), grid=(amount // dept...]
    all_gather x4 -> x3, waiting for transfers between devices: 193 us -> 171 us  [the longest x1 85.6 us: per_device(): feat_p = lax.all_gather(mine, 'ex', axis=1, tiled=True)]
    slice x5 -> x0, local copies, waits for them, and re-layouts: 6.66 us -> none  [the longest x4 5.24 us: hash_table(): mixed = mixed * (hash_words[0] | 1) + hash_words[1]]
  transfers between devices with their start and end apart: 5 -> 7, of which waited for: 5 -> 6; matrix products, arithmetic and copies ran while one was open for 1% -> 4% of each run, Pallas kernels for 0% -> 0%
where the time goes in v1:
time: 388 us
  waiting for transfers between devices  324 us (84%)
  Pallas kernels  24 us (6%)
  matrix products  18.3 us (5%)
  between operations  13.5 us (3%)
    all_gather x1, waiting for transfers between devices, per_device(): feat_p = lax.all_gather(mine, 'ex', axis=1, tiled=True)  85.6 us
    all_gather x1, waiting for transfers between devices, per_device(): everyone = lax.all_gather(gradients, 'ex', axis=0, tiled=True)  77.7 us
    reduce_scatter x1, waiting for transfers between devices, per_device(): scores = lax.psum_scatter(scores, 'ex', scatter_dimension=1, tiled=True)  62.2 us
    reduce_scatter x1, waiting for transfers between devices, per_device(): lax.psum_scatter(parts, 'par', scatter_dimension=0, tiled=True)  47 us
    reduce_scatter x1, waiting for transfers between devices, per_device(): summed = lax.psum_scatter(partial, 'par', scatter_dimension=1, tiled=True)  43.1 us
    pallas_call x1, Pallas kernels, project(): pl.pallas_call(functools.partial(hash_kernel, tile), grid=(amount // dept...  24 us
    dot_general x1, matrix products, per_device(): parts = jnp.dot(feat_p, inverse_gram, preferred_element_type=jnp.float32)  14.9 us
  transfers between devices with their start and end apart: 7, of which 6 were waited for; matrix products, arithmetic and copies ran while one was open for 4% of the time, Pallas kernels for 0%

profile of v1, /device:TPU:0, one launch (start us, length us, event | category | flops | bytes accessed | tf_op | source)
XLA Modules:
  0.0 388.2 jit_solution(14749620371924358665)
XLA Ops:
  6.5 0.0 all-gather.4.cloned.1.call-start
  6.5 0.7 all-gather.4.cloned.1.call-update
  7.3 0.0 reduce-scatter.4.cloned.1.call-start
  7.3 77.7 %all-gather.4.cloned.1.call-done.grads_ref = bf16[512,4096]{1,0:T(8,128)(2,1)} async-done(((bf16[64,4096]{1,0:T(8,128)(2,1)}), bf16[512,4096]{1,0:T(8,128)(2,1)}) %all-gather.4.cloned.1.call-update) | async-done | bytes 4194320 | tf_op jit(solution)/shard_map/all_gather | solution.py:71
  85.0 0.0 copy-start.1
  85.0 0.7 copy-done.1
  85.7 24.0 %shard_map.37 = f32[512,2048]{1,0:T(8,128)S(1)} custom-call(s32[4]{0:T(128)S(1)} %copy-done.1, s32[1]{0:T(128)} %bitcast.start_ref, s32[1,2048]{1,0:T(1,128)S(1)} %fusion.2.cols_ref, bf16[512,4096]{1,0:T(8,128)(2,1)} %all-gather.4.cloned.1.call-done.grads_ref), custom_call_target="tpu_custom_call" | custom-call | tf_op jit(solution)/shard_map/pallas_call | solution.py:47
  109.7 0.0 copy-start
  109.7 1.9 copy-done
  111.6 0.0 reduce-scatter.4.cloned.1.call-update
  111.6 0.0 all-gather.6.cloned.1.call-start
  111.7 43.1 %reduce-scatter.4.cloned.1.call-done = f32[512,512]{1,0:T(8,128)} async-done(((f32[512,2048]{1,0:T(8,128)}), f32[512,512]{1,0:T(8,128)}) %reduce-scatter.4.cloned.1.call-update) | async-done | bytes 1048592 | tf_op jit(solution)/shard_map/reduce_scatter | solution.py:73
  154.7 2.2 multiply_convert_fusion
  156.9 0.0 all-gather.6.cloned.1.call-update
  156.9 0.0 all-gather.8.cloned.1.call-start
  157.0 1.7 collective-permute-start
  158.7 0.0 collective-permute-done
  158.7 0.0 copy-start.2
  158.7 0.8 copy-done.2
  159.5 0.0 all-gather.8.cloned.1.call-update
  159.5 0.0 reduce-scatter.6.cloned.1.call-start
  159.6 85.6 %all-gather.6.cloned.1.call-done = bf16[512,4096]{1,0:T(8,128)(2,1)} async-done(((bf16[512,512]{1,0:T(8,128)(2,1)}), bf16[512,4096]{1,0:T(8,128)(2,1)}) %all-gather.6.cloned.1.call-update) | async-done | bytes 4194320 | tf_op jit(solution)/shard_map/all_gather | solution.py:75
  245.2 14.9 %fusion.5 = f32[512,2048]{1,0:T(8,128)} fusion(bf16[512,4096]{1,0:T(8,128)(2,1)} %all-gather.6.cloned.1.call-done, bf16[4096,2048]{1,0:T(8,128)(2,1)} %param.4), kind=kOutput, calls=%fused_computation.12 | convolution fusion | flops 8589934592 | bytes 25165824 | tf_op jit(solution)/shard_map/dot_general | solution.py:82
  260.1 0.0 reduce-scatter.6.cloned.1.call-update
  260.2 0.0 reduce-scatter.8.cloned.1.call-start
  260.2 7.2 %all-gather.8.cloned.1.call-done = bf16[512,2048]{1,0:T(8,128)(2,1)} async-done(((bf16[512,512]{1,0:T(8,128)(2,1)}), bf16[512,2048]{1,0:T(8,128)(2,1)}) %all-gather.8.cloned.1.call-update) | async-done | bytes 2097168 | tf_op jit(solution)/shard_map/all_gather | solution.py:81
  267.4 47.0 %reduce-scatter.6.cloned.1.call-done = f32[128,2048]{1,0:T(8,128)} async-done(((f32[512,2048]{1,0:T(8,128)}), f32[128,2048]{1,0:T(8,128)}) %reduce-scatter.6.cloned.1.call-update) | async-done | bytes 1048592 | tf_op jit(solution)/shard_map/reduce_scatter | solution.py:83
  314.4 3.4 fusion
  317.8 0.0 reduce-scatter.8.cloned.1.call-update
  317.8 62.2 %reduce-scatter.8.cloned.1.call-done = f32[128,64]{0,1:T(8,128)} async-done(((f32[128,512]{0,1:T(8,128)}), f32[128,64]{0,1:T(8,128)}) %reduce-scatter.8.cloned.1.call-update) | async-done | bytes 32784 | tf_op jit(solution)/shard_map/reduce_scatter | solution.py:90
  380.0 1.4 broadcast_multiply_fusion
  (1 shorter events, 0.0 us)
Async XLA Ops:
  6.5 78.5 %all-gather.4.cloned.1.call-start = ((), (), s32[]{:S(2)}) async-start(), calls=%async_computation.3 | async-start | bytes 4718592 | tf_op jit(solution)/shard_map/all_gather | solution.py:71
  7.3 147.5 %reduce-scatter.4.cloned.1.call-start = ((), (), s32[]{:S(2)}) async-start(), calls=%async_computation.4 | async-start | bytes 5242880 | tf_op jit(solution)/shard_map/reduce_scatter | solution.py:73
  85.0 0.7 copy-start.1
  109.7 1.9 copy-start
  111.6 133.6 %all-gather.6.cloned.1.call-start = ((), (), s32[]{:S(2)}) async-start(), calls=%async_computation.5 | async-start | bytes 4718592 | tf_op jit(solution)/shard_map/all_gather | solution.py:75
  156.9 110.5 %all-gather.8.cloned.1.call-start = ((), (), s32[]{:S(2)}) async-start(), calls=%async_computation.7 | async-start | bytes 2621440 | tf_op jit(solution)/shard_map/all_gather | solution.py:81
  157.0 1.7 collective-permute-start
  158.7 0.8 copy-start.2
  159.5 154.9 %reduce-scatter.6.cloned.1.call-start = ((), (), s32[]{:S(2)}) async-start(), calls=%async_computation.6 | async-start | bytes 5242880 | tf_op jit(solution)/shard_map/reduce_scatter | solution.py:83
  260.2 119.8 %reduce-scatter.8.cloned.1.call-start = ((), (), s32[]{:S(2)}) async-start(), calls=%async_computation.8 | async-start | bytes 294912 | tf_op jit(solution)/shard_map/reduce_scatter | solution.py:90
Sparse Core Ops, SparseCore 0:
  9.5 75.5 all-gather.3
  111.8 42.9 reduce-scatter.3
  157.1 88.1 all-gather.5
  246.6 20.7 all-gather.7
  269.8 44.5 reduce-scatter.5
  317.9 61.9 reduce-scatter.7

commit v2 on v1

--- a/solution.py
+++ b/solution.py
@@ -61,6 +61,165 @@
     )(words, start, cols, grads)
 
 
+MESH = pl.DeviceIdType.MESH
+
+
+def gather_kernel(ex_n, own_ref, out_ref, keep_sem, up_sem, down_sem, side_sem, recv_sem):
+    e = lax.axis_index("ex")
+    line, side = e // 2, e % 2
+    last = ex_n // 2 - 1
+    above, below, beside = lax.rem(e + 2, ex_n), lax.rem(e + ex_n - 2, ex_n), line * 2 + 1 - side
+    barrier = pltpu.get_barrier_semaphore()
+
+    def greet(peer):
+        pl.semaphore_signal(barrier, inc=1, device_id={"ex": peer}, device_id_type=MESH)
+
+    greet(beside)
+    pl.when(line < last)(lambda: greet(above))
+    pl.when(line > 0)(lambda: greet(below))
+    inside = (line > 0) & (line < last)
+    pl.when(inside)(lambda: pl.semaphore_wait(barrier, 3))
+    pl.when(jnp.logical_not(inside))(lambda: pl.semaphore_wait(barrier, 2))
+
+    def copy(src, slot, sems, peer):
+        return pltpu.make_async_remote_copy(
+            src_ref=src,
+            dst_ref=out_ref.at[slot],
+            send_sem=sems.at[slot],
+            recv_sem=recv_sem.at[slot],
+            device_id={"ex": peer},
+            device_id_type=MESH,
+        )
+
+    keep = pltpu.make_async_copy(own_ref, out_ref.at[e], keep_sem)
+    keep.start()
+    pl.when(line < last)(lambda: copy(own_ref, e, up_sem, above).start())
+    pl.when(line > 0)(lambda: copy(own_ref, e, down_sem, below).start())
+    copy(own_ref, e, side_sem, beside).start()
+    for far in range(1, last + 1):
+        low, high = e - 2 * far, e + 2 * far
+
+        @pl.when(line >= far)
+        def _():
+            copy(out_ref.at[low], low, up_sem, above).wait_recv()
+            pl.when(line < last)(lambda: copy(out_ref.at[low], low, up_sem, above).start())
+            copy(out_ref.at[low], low, side_sem, beside).start()
+
+        @pl.when(line + far <= last)
+        def _():
+            copy(out_ref.at[high], high, down_sem, below).wait_recv()
+            pl.when(line > 0)(lambda: copy(out_ref.at[high], high, down_sem, below).start())
+            copy(out_ref.at[high], high, side_sem, beside).start()
+
+    for spot in range(last + 1):
+        mine, other = 2 * spot + side, 2 * spot + 1 - side
+        copy(out_ref.at[other], other, side_sem, beside).wait_recv()
+        copy(out_ref.at[mine], mine, side_sem, beside).wait_send()
+
+        @pl.when((line < last) & (line >= spot))
+        def _():
+            copy(out_ref.at[mine], mine, up_sem, above).wait_send()
+
+        @pl.when((line > 0) & (line <= spot))
+        def _():
+            copy(out_ref.at[mine], mine, down_sem, below).wait_send()
+
+    keep.wait()
+
+
+def gather(ex_n, own, collective_id):
+    return pl.pallas_call(
+        functools.partial(gather_kernel, ex_n),
+        in_specs=[pl.BlockSpec(memory_space=pltpu.VMEM)],
+        out_specs=pl.BlockSpec(memory_space=pl.ANY),
+        out_shape=jax.ShapeDtypeStruct((ex_n,) + own.shape, own.dtype),
+        scratch_shapes=[pltpu.SemaphoreType.DMA]
+        + [pltpu.SemaphoreType.DMA((ex_n,)) for _ in range(4)],
+        compiler_params=pltpu.CompilerParams(
+            collective_id=collective_id, has_side_effects=True, vmem_limit_bytes=8 << 20
+        ),
+    )(own)
+
+
+def scatter_kernel(ex_n, scale, in_ref, out_ref, landed, send_sem, recv_sem):
+    e = lax.axis_index("ex")
+    rows = out_ref.shape[0]
+    barrier = pltpu.get_barrier_semaphore()
+    for far in range(1, ex_n):
+        peer = lax.rem(e + far, ex_n)
+        pl.semaphore_signal(barrier, inc=1, device_id={"ex": peer}, device_id_type=MESH)
+    pl.semaphore_wait(barrier, ex_n - 1)
+    copies = []
+    for far in range(1, ex_n):
+        peer = lax.rem(e + far, ex_n)
+        copies.append(
+            pltpu.make_async_remote_copy(
+                src_ref=in_ref.at[pl.ds(pl.multiple_of(peer * rows, rows), rows)],
+                dst_ref=landed.at[far],
+                send_sem=send_sem.at[far],
+                recv_sem=recv_sem.at[far],
+                device_id={"ex": peer},
+                device_id_type=MESH,
+            )
+        )
+        copies[-1].start()
+    total = in_ref[pl.ds(pl.multiple_of(e * rows, rows), rows), :]
+    for far in range(1, ex_n):
+        copies[far - 1].wait_recv()
+        total += landed[far]
+    out_ref[...] = total * scale
+    for each in copies:
+        each.wait_send()
+
+
+def scatter(ex_n, scale, stacked, collective_id):
+    rows, columns = stacked.shape[0] // ex_n, stacked.shape[1]
+    return pl.pallas_call(
+        functools.partial(scatter_kernel, ex_n, scale),
+        in_specs=[pl.BlockSpec(memory_space=pltpu.VMEM)],
+        out_specs=pl.BlockSpec(memory_space=pltpu.VMEM),
+        out_shape=jax.ShapeDtypeStruct((rows, columns), jnp.float32),
+        scratch_shapes=[
+            pltpu.VMEM((ex_n, rows, columns), jnp.float32),
+            pltpu.SemaphoreType.DMA((ex_n,)),
+            pltpu.SemaphoreType.DMA((ex_n,)),
+        ],
+        compiler_params=pltpu.CompilerParams(
+            collective_id=collective_id, has_side_effects=True, vmem_limit_bytes=16 << 20
+        ),
+    )(stacked)
+
+
+def tiles_kernel(feat_ref, gram_ref, out_ref):
+    part = jnp.dot(feat_ref[0], gram_ref[...], preferred_element_type=jnp.float32)
+
+    @pl.when(pl.program_id(0) == 0)
+    def _():
+        out_ref[...] = part
+
+    @pl.when(pl.program_id(0) > 0)
+    def _():
+        out_ref[...] += part
+
+
+def precondition(blocks, gram):
+    count, rows, piece = blocks.shape
+    width = gram.shape[1]
+    return pl.pallas_call(
+        tiles_kernel,
+        grid=(count,),
+        in_specs=[
+            pl.BlockSpec((1, rows, piece), lambda k: (k, 0, 0)),
+            pl.BlockSpec((piece, width), lambda k: (k, 0)),
+        ],
+        out_specs=pl.BlockSpec((rows, width), lambda k: (0, 0)),
+        out_shape=jax.ShapeDtypeStruct((rows, width), jnp.float32),
+        compiler_params=pltpu.CompilerParams(
+            dimension_semantics=("arbitrary",), vmem_limit_bytes=48 << 20
+        ),
+    )(blocks, gram)
+
+
 def per_device(ex_n, par_n, gradients, inverse_gram, hash_words):
     amount = gradients.shape[1]
     feat_par, feat_ex = inverse_gram.shape
@@ -68,27 +227,26 @@
     e, p = lax.axis_index("ex"), lax.axis_index("par")
     ids = jnp.arange(feat_ex, dtype=jnp.int32)
     cols = (ids // piece) * feat_par + e * piece + ids % piece
-    everyone = lax.all_gather(gradients, "ex", axis=0, tiled=True)
+    everyone = gather(ex_n, gradients, 1).reshape(-1, amount)
     partial = project(hash_words, (p * amount)[None], cols[None, :], everyone)
     summed = lax.psum_scatter(partial, "par", scatter_dimension=1, tiled=True)
     mine = (summed * FEATURES ** (-0.5)).astype(jnp.bfloat16)
-    feat_p = lax.all_gather(mine, "ex", axis=1, tiled=True)
     pairs = []
     for src_e in range(ex_n):
         for src_p in range(par_n):
             pairs.append((src_e * par_n + src_p, src_p * ex_n + src_e))
     moved = lax.ppermute(mine, ("ex", "par"), pairs)
     feat_e = lax.all_gather(moved, "par", axis=1, tiled=True)
-    parts = jnp.dot(feat_p, inverse_gram, preferred_element_type=jnp.float32)
+    blocks = gather(ex_n, mine, 2)
+    parts = precondition(blocks, inverse_gram)
     conditioned = lax.psum_scatter(parts, "par", scatter_dimension=0, tiled=True)
-    scores = lax.dot_general(
+    turned = lax.dot_general(
+        feat_e,
         conditioned.astype(jnp.bfloat16),
-        feat_e,
         (((1,), (1,)), ((), ())),
         preferred_element_type=jnp.float32,
     )
-    scores = lax.psum_scatter(scores, "ex", scatter_dimension=1, tiled=True)
-    return scores * FEATURES ** (-0.5)
+    return scatter(ex_n, FEATURES ** (-0.5), turned, 3).T
 
 
 def solution(mesh):

time: 388 us -> 293 us (0.76)
  waiting for transfers between devices: 324 us -> 88 us
  Pallas kernels: 24 us -> 176 us
  matrix products: 18.3 us -> 2.57 us
  local copies, waits for them, and re-layouts: 3.4 us -> 10.2 us
    all_gather x2 -> x0, waiting for transfers between devices: 163 us -> none  [the longest x1 85.6 us: per_device(): feat_p = lax.all_gather(mine, 'ex', axis=1, tiled=True)]
    pallas_call x0 -> x4, Pallas kernels: none -> 152 us  [the longest x2 128 us: gather(): pl.pallas_call(functools.partial(gather_kernel, ex_n), in_specs=[pl.Block...]
    reduce_scatter x1 -> x0, waiting for transfers between devices: 62.2 us -> none  [per_device(): scores = lax.psum_scatter(scores, 'ex', scatter_dimension=1, tiled=True)]
    dot_general x2 -> x1, matrix products: 18.3 us -> 2.57 us  [per_device(): lax.dot_general(feat_e, conditioned.astype(jnp.bfloat16), (((1,), (1,)),...]
    all_gather x1, waiting for transfers between devices: 7.2 us -> 0.02 us  [per_device(): feat_e = lax.all_gather(moved, 'par', axis=1, tiled=True)]
    unnamed x6 -> x15, local copies, waits for them, and re-layouts: 3.4 us -> 10.2 us
  transfers between devices with their start and end apart: 7 -> 4, of which waited for: 6 -> 2; matrix products, arithmetic and copies ran while one was open for 4% -> 0% of each run, Pallas kernels for 0% -> 31%
where the time goes in v2:
time: 293 us; the launch traced here: 292 us
  Pallas kernels  176 us (60%)
  waiting for transfers between devices  88 us (30%)
  between operations  13.2 us (5%)
  local copies, waits for them, and re-layouts  10.2 us (3%)
    pallas_call x2, Pallas kernels, gather(): pl.pallas_call(functools.partial(gather_kernel, ex_n), in_specs=[pl.Block...  128 us
    reduce_scatter x1, waiting for transfers between devices, per_device(): lax.psum_scatter(parts, 'par', scatter_dimension=0, tiled=True)  45.1 us
    reduce_scatter x1, waiting for transfers between devices, per_device(): summed = lax.psum_scatter(partial, 'par', scatter_dimension=1, tiled=True)  42.9 us
    pallas_call x1, Pallas kernels, project(): pl.pallas_call(functools.partial(hash_kernel, tile), grid=(amount // dept...  24 us
    pallas_call x1, Pallas kernels, precondition(): pl.pallas_call(tiles_kernel, grid=(count,), in_specs=[pl.BlockSpec((1, ro...  15.3 us
    unnamed x15, local copies, waits for them, and re-layouts  10.2 us
    pallas_call x1, Pallas kernels, scatter(): pl.pallas_call(functools.partial(scatter_kernel, ex_n, scale), in_specs=[...  8.88 us
  transfers between devices with their start and end apart: 4, of which 2 were waited for; matrix products, arithmetic and copies ran while one was open for 0% of the time, Pallas kernels for 31%

profile of v2, /device:TPU:0, one launch (start us, length us, event | category | flops | bytes accessed | tf_op | source)
XLA Modules:
  0.0 292.3 jit_solution(5653308647122112594)
XLA Ops:
  6.5 0.0 copy-start.5
  6.5 0.0 reduce-scatter.3.cloned.1.call-start
  6.6 0.0 copy-start.4
  6.6 1.0 copy-done.4
  7.6 52.5 %shard_map.37 = bf16[8,64,4096]{2,1,0:T(8,128)(2,1)S(1)} custom-call(bf16[64,4096]{1,0:T(8,128)(2,1)S(1)} %copy-done.4), custom_call_target="tpu_custom_call" | custom-call | tf_op jit(solution)/shard_map/pallas_call | solution.py:131
  60.1 0.0 copy-start
  60.1 1.9 copy-done
  62.1 0.0 copy-done.5
  62.1 24.0 %shard_map.38 = f32[512,2048]{1,0:T(8,128)S(1)} custom-call(s32[4]{0:T(128)S(1)} %copy-done.5, s32[1]{0:T(128)} %bitcast.start_ref, s32[1,2048]{1,0:T(1,128)S(1)} %fusion.2.cols_ref, bf16[512,4096]{1,0:T(8,128)(2,1)} %bitcast.4), custom_call_target="tpu_custom_call" | custom-call | tf_op jit(solution)/shard_map/pallas_call | solution.py:47
  86.0 0.0 copy-start.1
  86.1 1.9 copy-done.1
  88.0 0.0 reduce-scatter.3.cloned.1.call-update
  88.0 0.0 all-gather.2.cloned.1.call-start
  88.1 42.9 %reduce-scatter.3.cloned.1.call-done = f32[512,512]{1,0:T(8,128)} async-done(((f32[512,2048]{1,0:T(8,128)}), f32[512,512]{1,0:T(8,128)}) %reduce-scatter.3.cloned.1.call-update) | async-done | bytes 1048592 | tf_op jit(solution)/shard_map/reduce_scatter | solution.py:232
  131.0 1.3 multiply_convert_fusion.own_ref
  132.3 0.7 collective-permute-start
  133.0 0.0 collective-permute-done
  133.0 0.0 copy-start.6
  133.0 0.8 copy-done.6
  133.8 0.0 all-gather.2.cloned.1.call-update
  133.8 0.0 reduce-scatter.5.cloned.1.call-start
  133.9 75.4 %shard_map.39.feat_ref = bf16[8,512,512]{2,1,0:T(8,128)(2,1)S(1)} custom-call(bf16[512,512]{1,0:T(8,128)(2,1)S(1)} %multiply_convert_fusion.own_ref), custom_call_target="tpu_custom_call" | custom-call | tf_op jit(solution)/shard_map/pallas_call | solution.py:131
  209.3 0.0 copy-start.3
  209.4 1.9 copy-done.3
  211.3 15.3 %shard_map.40 = f32[512,2048]{1,0:T(8,128)S(1)} custom-call(bf16[8,512,512]{2,1,0:T(8,128)(2,1)} %copy-done.3, bf16[4096,2048]{1,0:T(8,128)(2,1)} %gram_ref.1), custom_call_target="tpu_custom_call" | custom-call | tf_op jit(solution)/shard_map/pallas_call | solution.py:208
  226.6 0.0 copy-start.2
  226.6 1.9 copy-done.2
  228.5 0.0 reduce-scatter.5.cloned.1.call-update
  228.5 0.0 all-gather.2.cloned.1.call-done
  228.6 45.1 %reduce-scatter.5.cloned.1.call-done = f32[128,2048]{1,0:T(8,128)} async-done(((f32[512,2048]{1,0:T(8,128)}), f32[128,2048]{1,0:T(8,128)}) %reduce-scatter.5.cloned.1.call-update) | async-done | bytes 1048592 | tf_op jit(solution)/shard_map/reduce_scatter | solution.py:242
  273.6 2.6 fusion.in_ref
  276.2 8.9 %shard_map.41 = f32[64,128]{1,0:T(8,128)S(1)} custom-call(f32[512,128]{1,0:T(8,128)S(1)} %fusion.in_ref), custom_call_target="tpu_custom_call" | custom-call | tf_op jit(solution)/shard_map/pallas_call | solution.py:177
  285.1 0.6 copy.5
  (1 shorter events, 0.0 us)
Async XLA Ops:
  6.5 55.5 %copy-start.5 = (s32[4]{0:T(128)S(1)}, s32[4]{0:T(128)}, u32[]{:S(2)}) copy-start(s32[4]{0:T(128)} %words_ref.1) | copy-start | bytes 52
  6.5 124.4 %reduce-scatter.3.cloned.1.call-start = ((), (), s32[]{:S(2)}) async-start(), calls=%async_computation.2 | async-start | bytes 5242880 | tf_op jit(solution)/shard_map/reduce_scatter | solution.py:232
  6.6 1.0 copy-start.4
  60.1 2.0 copy-start
  86.0 2.0 copy-start.1
  88.0 140.5 %all-gather.2.cloned.1.call-start = ((), (), s32[]{:S(2)}) async-start(), calls=%async_computation.3 | async-start | bytes 2621440 | tf_op jit(solution)/shard_map/all_gather | solution.py:239
  132.3 0.7 collective-permute-start
  133.0 0.8 copy-start.6
  133.8 139.8 %reduce-scatter.5.cloned.1.call-start = ((), (), s32[]{:S(2)}) async-start(), calls=%async_computation.4 | async-start | bytes 5242880 | tf_op jit(solution)/shard_map/reduce_scatter | solution.py:242
  209.3 2.0 copy-start.3
  226.6 2.0 copy-start.2
Sparse Core Ops, SparseCore 0:
  88.2 42.7 reduce-scatter.2
  134.0 48.8 all-gather.1
  228.7 44.9 reduce-scatter.4

commit v3 on v2

--- a/solution.py
+++ b/solution.py
@@ -23,7 +23,8 @@
     row_base = (start_ref[0] + step * depth) * FEATURES * m0 + words_ref[1]
     rows = lax.broadcasted_iota(jnp.int32, (depth, tile), 0) * (m0 * FEATURES)
     grads = grads_ref[...]
-    for first in range(0, out_ref.shape[1], tile):
+    for spot in range(out_ref.shape[0]):
+        first = spot * tile
         mixed = rows + (cols_ref[:, first:first + tile] * m0 + row_base)
         mixed = (mixed ^ shifted(mixed, 15)) * m2
         mixed = (mixed ^ shifted(mixed, 13)) * m3
@@ -32,18 +33,17 @@
 
         @pl.when(step == 0)
         def _():
-            out_ref[:, first:first + tile] = part
+            out_ref[spot] = part
 
         @pl.when(step > 0)
         def _():
-            out_ref[:, first:first + tile] += part
-
-
-def project(words, start, cols, grads):
+            out_ref[spot] += part
+
+
+def project(words, start, cols, grads, tile):
     rows, amount = grads.shape
     width = cols.shape[1]
     depth = min(512, amount)
-    tile = min(512, width)
     return pl.pallas_call(
         functools.partial(hash_kernel, tile),
         grid=(amount // depth,),
@@ -53,8 +53,8 @@
             pl.BlockSpec((1, width), lambda k: (0, 0)),
             pl.BlockSpec((rows, depth), lambda k: (0, k)),
         ],
-        out_specs=pl.BlockSpec((rows, width), lambda k: (0, 0)),
-        out_shape=jax.ShapeDtypeStruct((rows, width), jnp.float32),
+        out_specs=pl.BlockSpec((width // tile, rows, tile), lambda k: (0, 0, 0)),
+        out_shape=jax.ShapeDtypeStruct((width // tile, rows, tile), jnp.float32),
         compiler_params=pltpu.CompilerParams(
             dimension_semantics=("arbitrary",), vmem_limit_bytes=48 << 20
         ),
@@ -190,6 +190,73 @@
     )(stacked)
 
 
+def fold_kernel(chips, cuts, scale, in_ref, out_ref, near, staged, landed, near_send, near_recv, far_send, far_recv):
+    p = lax.axis_index("par")
+    x, core = p // 2, p % 2
+    rows = in_ref.shape[1] // cuts
+    partner = x * 2 + 1 - core
+    barrier = pltpu.get_barrier_semaphore()
+    pl.semaphore_signal(barrier, inc=1, device_id={"par": partner}, device_id_type=MESH)
+    for d in range(1, chips):
+        peer = lax.rem(x + d, chips) * 2 + core
+        pl.semaphore_signal(barrier, inc=1, device_id={"par": peer}, device_id_type=MESH)
+    pl.semaphore_wait(barrier, chips)
+    order = [(d, c) for d in list(range(1, chips)) + [0] for c in range(cuts)]
+    across, onward = {}, {}
+    for d, c in order:
+        part = pl.ds(c * rows, rows)
+        across[d, c] = pltpu.make_async_remote_copy(
+            src_ref=in_ref.at[lax.rem(x + d, chips) * 2 + 1 - core, part],
+            dst_ref=near.at[d, part],
+            send_sem=near_send.at[d, c],
+            recv_sem=near_recv.at[d, c],
+            device_id={"par": partner},
+            device_id_type=MESH,
+        )
+        across[d, c].start()
+    for d, c in order:
+        part = pl.ds(c * rows, rows)
+        across[d, c].wait_recv()
+        total = in_ref[lax.rem(x + d, chips) * 2 + core, part, :] + near[d, part, :]
+        staged[d, part, :] = total
+        if d > 0:
+            onward[d, c] = pltpu.make_async_remote_copy(
+                src_ref=staged.at[d, part],
+                dst_ref=landed.at[d, part],
+                send_sem=far_send.at[d, c],
+                recv_sem=far_recv.at[d, c],
+                device_id={"par": lax.rem(x + d, chips) * 2 + core},
+                device_id_type=MESH,
+            )
+            onward[d, c].start()
+    for c in range(cuts):
+        part = pl.ds(c * rows, rows)
+        total = staged[0, part, :]
+        for d in range(1, chips):
+            onward[d, c].wait_recv()
+            total += landed[d, part, :]
+        out_ref[part, :] = (total * scale).astype(out_ref.dtype)
+    for each in list(across.values()) + list(onward.values()):
+        each.wait_send()
+
+
+def fold(scale, stacked, collective_id):
+    par_n, rows, columns = stacked.shape
+    chips, cuts = par_n // 2, 4
+    hold = pltpu.VMEM((chips, rows, columns), jnp.float32)
+    return pl.pallas_call(
+        functools.partial(fold_kernel, chips, cuts, scale),
+        in_specs=[pl.BlockSpec(memory_space=pltpu.VMEM)],
+        out_specs=pl.BlockSpec(memory_space=pltpu.VMEM),
+        out_shape=jax.ShapeDtypeStruct((rows, columns), jnp.bfloat16),
+        scratch_shapes=[hold, hold, hold]
+        + [pltpu.SemaphoreType.DMA((chips, cuts)) for _ in range(4)],
+        compiler_params=pltpu.CompilerParams(
+            collective_id=collective_id, has_side_effects=True, vmem_limit_bytes=48 << 20
+        ),
+    )(stacked)
+
+
 def tiles_kernel(feat_ref, gram_ref, out_ref):
     part = jnp.dot(feat_ref[0], gram_ref[...], preferred_element_type=jnp.float32)
 
@@ -217,6 +284,11 @@
         compiler_params=pltpu.CompilerParams(
             dimension_semantics=("arbitrary",), vmem_limit_bytes=48 << 20
         ),
+        cost_estimate=pl.CostEstimate(
+            flops=2 * count * rows * piece * width,
+            bytes_accessed=2 * count * piece * (rows + width) + 4 * rows * width,
+            transcendentals=0,
+        ),
     )(blocks, gram)
 
 
@@ -228,21 +300,21 @@
     ids = jnp.arange(feat_ex, dtype=jnp.int32)
     cols = (ids // piece) * feat_par + e * piece + ids % piece
     everyone = gather(ex_n, gradients, 1).reshape(-1, amount)
-    partial = project(hash_words, (p * amount)[None], cols[None, :], everyone)
-    summed = lax.psum_scatter(partial, "par", scatter_dimension=1, tiled=True)
-    mine = (summed * FEATURES ** (-0.5)).astype(jnp.bfloat16)
+    partial = project(hash_words, (p * amount)[None], cols[None, :], everyone, piece)
+    mine = fold(FEATURES ** (-0.5), partial, 4)
+    blocks = gather(ex_n, mine, 2)
+    mine, blocks = lax.optimization_barrier((mine, blocks))
     pairs = []
     for src_e in range(ex_n):
         for src_p in range(par_n):
             pairs.append((src_e * par_n + src_p, src_p * ex_n + src_e))
     moved = lax.ppermute(mine, ("ex", "par"), pairs)
     feat_e = lax.all_gather(moved, "par", axis=1, tiled=True)
-    blocks = gather(ex_n, mine, 2)
     parts = precondition(blocks, inverse_gram)
-    conditioned = lax.psum_scatter(parts, "par", scatter_dimension=0, tiled=True)
+    conditioned = fold(1.0, parts.reshape(par_n, -1, feat_ex), 5)
     turned = lax.dot_general(
         feat_e,
-        conditioned.astype(jnp.bfloat16),
+        conditioned,
         (((1,), (1,)), ((), ())),
         preferred_element_type=jnp.float32,
     )

time: 293 us -> 255 us (0.87)
  waiting for transfers between devices: 88 us -> 0.04 us
  Pallas kernels: 176 us -> 231 us
  local copies, waits for them, and re-layouts: 10.2 us -> 6.32 us
    reduce_scatter x2 -> x0, waiting for transfers between devices: 87.9 us -> none  [the longest x1 45.1 us: per_device(): lax.psum_scatter(parts, 'par', scatter_dimension=0, tiled=True)]
    pallas_call x0 -> x2, Pallas kernels: none -> 81.3 us  [fold(): pl.pallas_call(functools.partial(fold_kernel, chips, cuts, scale), in_spe...]
    pallas_call x2, Pallas kernels: 128 us -> 102 us  [gather(): pl.pallas_call(functools.partial(gather_kernel, ex_n), in_specs=[pl.Block...]
    unnamed x15 -> x11, local copies, waits for them, and re-layouts: 10.2 us -> 6.32 us
  transfers between devices with their start and end apart: 4 -> 2, of which waited for: 2 -> 0; matrix products, arithmetic and copies ran while one was open for 0% -> 0% of each run, Pallas kernels for 31% -> 27%
where the time goes in v3:
time: 255 us; the launch traced here: 254 us
  Pallas kernels  231 us (91%)
  between operations  13.5 us (5%)
  local copies, waits for them, and re-layouts  6.32 us (2%)
    pallas_call x2, Pallas kernels, gather(): pl.pallas_call(functools.partial(gather_kernel, ex_n), in_specs=[pl.Block...  102 us
    pallas_call x2, Pallas kernels, fold(): pl.pallas_call(functools.partial(fold_kernel, chips, cuts, scale), in_spe...  81.3 us
    pallas_call x1, Pallas kernels, project(): pl.pallas_call(functools.partial(hash_kernel, tile), grid=(amount // dept...  24 us
    pallas_call x1, Pallas kernels, precondition(): pl.pallas_call(tiles_kernel, grid=(count,), in_specs=[pl.BlockSpec((1, ro...  15.3 us
    pallas_call x1, Pallas kernels, scatter(): pl.pallas_call(functools.partial(scatter_kernel, ex_n, scale), in_specs=[...  9.24 us
    unnamed x11, local copies, waits for them, and re-layouts  6.32 us
  transfers between devices with their start and end apart: 2, of which 0 were waited for; matrix products, arithmetic and copies ran while one was open for 0% of the time, Pallas kernels for 27%

profile of v3, /device:TPU:0, one launch (start us, length us, event | category | flops | bytes accessed | tf_op | source)
XLA Modules:
  0.0 254.3 jit_solution(7364586244241755225)
XLA Ops:
  6.5 0.0 copy-start.3
  6.5 0.0 all-gather.2.cloned.1.call-start
  6.6 0.0 copy-start.2
  6.6 1.0 copy-done.2
  7.6 52.5 %shard_map.37 = bf16[8,64,4096]{2,1,0:T(8,128)(2,1)S(1)} custom-call(bf16[64,4096]{1,0:T(8,128)(2,1)S(1)} %copy-done.2), custom_call_target="tpu_custom_call" | custom-call | tf_op jit(solution)/shard_map/pallas_call | solution.py:131
  60.1 0.0 copy-start
  60.1 1.9 copy-done
  62.0 0.0 copy-done.3
  62.0 24.0 %shard_map.38.in_ref = f32[4,512,512]{2,1,0:T(8,128)S(1)} custom-call(s32[4]{0:T(128)S(1)} %copy-done.3, s32[1]{0:T(128)} %bitcast.start_ref, s32[1,2048]{1,0:T(1,128)S(1)} %fusion.cols_ref, bf16[512,4096]{1,0:T(8,128)(2,1)} %bitcast.6), custom_call_target="tpu_custom_call" | custom-call | tf_op jit(solution)/shard_map/pallas_call | solution.py:47
  86.0 27.3 %shard_map.39.own_ref = bf16[512,512]{1,0:T(8,128)(2,1)S(1)} custom-call(f32[4,512,512]{2,1,0:T(8,128)S(1)} %shard_map.38.in_ref), custom_call_target="tpu_custom_call" | custom-call | tf_op jit(solution)/shard_map/pallas_call | solution.py:247
  113.3 49.2 %shard_map.40.feat_ref = bf16[8,512,512]{2,1,0:T(8,128)(2,1)S(1)} custom-call(bf16[512,512]{1,0:T(8,128)(2,1)S(1)} %shard_map.39.own_ref), custom_call_target="tpu_custom_call" | custom-call | tf_op jit(solution)/shard_map/pallas_call | solution.py:131
  162.5 0.0 copy-start.1
  162.6 1.9 copy-done.1
  164.5 0.7 collective-permute-start
  165.2 0.0 collective-permute-done
  165.2 0.0 copy-start.4
  165.2 0.8 copy-done.4
  166.0 0.0 all-gather.2.cloned.1.call-update
  166.0 15.3 %shard_map.41 = f32[512,2048]{1,0:T(8,128)S(1)} custom-call(bf16[8,512,512]{2,1,0:T(8,128)(2,1)} %copy-done.1, bf16[4096,2048]{1,0:T(8,128)(2,1)} %gram_ref.1), custom_call_target="tpu_custom_call" | custom-call | flops 8589934592 | bytes 25165824 | tf_op jit(solution)/shard_map/pallas_call | solution.py:275
  181.3 54.0 %shard_map.42 = bf16[128,2048]{1,0:T(8,128)(2,1)S(1)} custom-call(f32[4,128,2048]{2,1,0:T(8,128)S(1)} %bitcast.7), custom_call_target="tpu_custom_call" | custom-call | tf_op jit(solution)/shard_map/pallas_call | solution.py:247
  235.3 0.0 all-gather.2.cloned.1.call-done
  235.3 2.3 fusion.3.in_ref
  237.6 9.2 %shard_map.43 = f32[64,128]{1,0:T(8,128)S(1)} custom-call(f32[512,128]{1,0:T(8,128)S(1)} %fusion.3.in_ref), custom_call_target="tpu_custom_call" | custom-call | tf_op jit(solution)/shard_map/pallas_call | solution.py:177
  246.9 0.6 copy.5
  (1 shorter events, 0.0 us)
Async XLA Ops:
  6.5 55.5 %copy-start.3 = (s32[4]{0:T(128)S(1)}, s32[4]{0:T(128)}, u32[]{:S(2)}) copy-start(s32[4]{0:T(128)} %words_ref.1) | copy-start | bytes 52
  6.5 228.8 %all-gather.2.cloned.1.call-start = ((), (), s32[]{:S(2)}) async-start(), calls=%async_computation | async-start | bytes 2621440 | tf_op jit(solution)/shard_map/all_gather | solution.py:312
  6.6 1.0 copy-start.2
  60.1 1.9 copy-start
  162.5 1.9 copy-start.1
  164.5 0.7 collective-permute-start
  165.2 0.8 copy-start.4
Sparse Core Ops, SparseCore 0:
  166.1 57.0 all-gather.1

commit v4 on v3

--- a/solution.py
+++ b/solution.py
@@ -240,7 +240,7 @@
         each.wait_send()
 
 
-def fold(scale, stacked, collective_id):
+def fold(scale, stacked, dtype, collective_id):
     par_n, rows, columns = stacked.shape
     chips, cuts = par_n // 2, 4
     hold = pltpu.VMEM((chips, rows, columns), jnp.float32)
@@ -248,7 +248,7 @@
         functools.partial(fold_kernel, chips, cuts, scale),
         in_specs=[pl.BlockSpec(memory_space=pltpu.VMEM)],
         out_specs=pl.BlockSpec(memory_space=pltpu.VMEM),
-        out_shape=jax.ShapeDtypeStruct((rows, columns), jnp.bfloat16),
+        out_shape=jax.ShapeDtypeStruct((rows, columns), dtype),
         scratch_shapes=[hold, hold, hold]
         + [pltpu.SemaphoreType.DMA((chips, cuts)) for _ in range(4)],
         compiler_params=pltpu.CompilerParams(
@@ -258,18 +258,22 @@
 
 
 def tiles_kernel(feat_ref, gram_ref, out_ref):
-    part = jnp.dot(feat_ref[0], gram_ref[...], preferred_element_type=jnp.float32)
-
-    @pl.when(pl.program_id(0) == 0)
-    def _():
-        out_ref[...] = part
-
-    @pl.when(pl.program_id(0) > 0)
-    def _():
-        out_ref[...] += part
-
-
-def precondition(blocks, gram):
+    step = pl.program_id(0)
+    tile = out_ref.shape[2]
+    for spot in range(out_ref.shape[0]):
+        gram = gram_ref[:, spot * tile:(spot + 1) * tile]
+        part = jnp.dot(feat_ref[0], gram, preferred_element_type=jnp.float32)
+
+        @pl.when(step == 0)
+        def _():
+            out_ref[spot] = part
+
+        @pl.when(step > 0)
+        def _():
+            out_ref[spot] += part
+
+
+def precondition(blocks, gram, tile):
     count, rows, piece = blocks.shape
     width = gram.shape[1]
     return pl.pallas_call(
@@ -279,8 +283,8 @@
             pl.BlockSpec((1, rows, piece), lambda k: (k, 0, 0)),
             pl.BlockSpec((piece, width), lambda k: (k, 0)),
         ],
-        out_specs=pl.BlockSpec((rows, width), lambda k: (0, 0)),
-        out_shape=jax.ShapeDtypeStruct((rows, width), jnp.float32),
+        out_specs=pl.BlockSpec((width // tile, rows, tile), lambda k: (0, 0, 0)),
+        out_shape=jax.ShapeDtypeStruct((width // tile, rows, tile), jnp.float32),
         compiler_params=pltpu.CompilerParams(
             dimension_semantics=("arbitrary",), vmem_limit_bytes=48 << 20
         ),
@@ -301,7 +305,7 @@
     cols = (ids // piece) * feat_par + e * piece + ids % piece
     everyone = gather(ex_n, gradients, 1).reshape(-1, amount)
     partial = project(hash_words, (p * amount)[None], cols[None, :], everyone, piece)
-    mine = fold(FEATURES ** (-0.5), partial, 4)
+    mine = fold(FEATURES ** (-0.5), partial, jnp.bfloat16, 4)
     blocks = gather(ex_n, mine, 2)
     mine, blocks = lax.optimization_barrier((mine, blocks))
     pairs = []
@@ -309,16 +313,16 @@
         for src_p in range(par_n):
             pairs.append((src_e * par_n + src_p, src_p * ex_n + src_e))
     moved = lax.ppermute(mine, ("ex", "par"), pairs)
-    feat_e = lax.all_gather(moved, "par", axis=1, tiled=True)
-    parts = precondition(blocks, inverse_gram)
-    conditioned = fold(1.0, parts.reshape(par_n, -1, feat_ex), 5)
-    turned = lax.dot_general(
-        feat_e,
+    parts = precondition(blocks, inverse_gram, piece)
+    conditioned = fold(1.0, parts, jnp.bfloat16, 5)
+    pairs = lax.dot_general(
         conditioned,
+        moved,
         (((1,), (1,)), ((), ())),
         preferred_element_type=jnp.float32,
     )
-    return scatter(ex_n, FEATURES ** (-0.5), turned, 3).T
+    rows = fold(1.0, pairs.reshape(par_n, -1, pairs.shape[1]), jnp.float32, 6)
+    return scatter(ex_n, FEATURES ** (-0.5), rows.T, 3).T
 
 
 def solution(mesh):

time: 255 us -> 228 us (0.89)
  between operations: 13.5 us -> 0.12 us
  Pallas kernels: 231 us -> 221 us
    pallas_call x2 -> x3, Pallas kernels: 81.3 us -> 66.7 us  [fold(): pl.pallas_call(functools.partial(fold_kernel, chips, cuts, scale), in_spe...]
    pallas_call x1, Pallas kernels: 15.3 us -> 18.8 us  [precondition(): pl.pallas_call(tiles_kernel, grid=(count,), in_specs=[pl.BlockSpec((1, ro...]
    unnamed x11 -> x9, local copies, waits for them, and re-layouts: 6.32 us -> 5.52 us
  transfers between devices with their start and end apart: 2 -> 1, of which waited for: 0 -> 0; matrix products, arithmetic and copies ran while one was open for 0% -> 0% of each run, Pallas kernels for 27% -> 21%
where the time goes in v4:
time: 228 us
  Pallas kernels  221 us (97%)
  local copies, waits for them, and re-layouts  5.64 us (2%)
    pallas_call x2, Pallas kernels, gather(): pl.pallas_call(functools.partial(gather_kernel, ex_n), in_specs=[pl.Block...  101 us
    pallas_call x3, Pallas kernels, fold(): pl.pallas_call(functools.partial(fold_kernel, chips, cuts, scale), in_spe...  66.7 us
    pallas_call x1, Pallas kernels, project(): pl.pallas_call(functools.partial(hash_kernel, tile), grid=(amount // dept...  23.9 us
    pallas_call x1, Pallas kernels, precondition(): pl.pallas_call(tiles_kernel, grid=(count,), in_specs=[pl.BlockSpec((1, ro...  18.8 us
    pallas_call x1, Pallas kernels, scatter(): pl.pallas_call(functools.partial(scatter_kernel, ex_n, scale), in_specs=[...  9.92 us
    unnamed x9, local copies, waits for them, and re-layouts  5.52 us
  transfers between devices with their start and end apart: 1, of which 0 were waited for; matrix products, arithmetic and copies ran while one was open for 0% of the time, Pallas kernels for 21%

profile of v4, /device:TPU:0, one launch (start us, length us, event | category | flops | bytes accessed | tf_op | source)
XLA Modules:
  0.0 227.8 jit_solution(7249573969543723013)
XLA Ops:
  0.0 0.0 copy-start.3
  0.0 0.0 copy-start.2
  0.0 1.0 copy-done.2
  1.1 52.5 %shard_map.37 = bf16[8,64,4096]{2,1,0:T(8,128)(2,1)S(1)} custom-call(bf16[64,4096]{1,0:T(8,128)(2,1)S(1)} %copy-done.2), custom_call_target="tpu_custom_call" | custom-call | tf_op jit(solution)/shard_map/pallas_call | solution.py:131
  53.6 0.0 copy-start
  53.6 1.9 copy-done
  55.5 0.0 copy-done.3
  55.5 23.9 %shard_map.38.in_ref = f32[4,512,512]{2,1,0:T(8,128)S(1)} custom-call(s32[4]{0:T(128)S(1)} %copy-done.3, s32[1]{0:T(128)} %bitcast.start_ref, s32[1,2048]{1,0:T(1,128)S(1)} %fusion.cols_ref, bf16[512,4096]{1,0:T(8,128)(2,1)} %bitcast.7), custom_call_target="tpu_custom_call" | custom-call | tf_op jit(solution)/shard_map/pallas_call | solution.py:47
  79.4 27.3 %shard_map.39.own_ref = bf16[512,512]{1,0:T(8,128)(2,1)S(1)} custom-call(f32[4,512,512]{2,1,0:T(8,128)S(1)} %shard_map.38.in_ref), custom_call_target="tpu_custom_call" | custom-call | tf_op jit(solution)/shard_map/pallas_call | solution.py:247
  106.7 49.0 %shard_map.40.feat_ref = bf16[8,512,512]{2,1,0:T(8,128)(2,1)S(1)} custom-call(bf16[512,512]{1,0:T(8,128)(2,1)S(1)} %shard_map.39.own_ref), custom_call_target="tpu_custom_call" | custom-call | tf_op jit(solution)/shard_map/pallas_call | solution.py:131
  155.7 0.0 copy-start.1
  155.7 1.9 copy-done.1
  157.7 0.7 collective-permute-start
  158.4 18.8 %shard_map.41.in_ref = f32[4,512,512]{2,1,0:T(8,128)S(1)} custom-call(bf16[8,512,512]{2,1,0:T(8,128)(2,1)} %copy-done.1, bf16[4096,2048]{1,0:T(8,128)(2,1)} %gram_ref.1), custom_call_target="tpu_custom_call" | custom-call | flops 8589934592 | bytes 25165824 | tf_op jit(solution)/shard_map/pallas_call | solution.py:279
  177.2 29.7 %shard_map.42 = bf16[512,512]{1,0:T(8,128)(2,1)S(1)} custom-call(f32[4,512,512]{2,1,0:T(8,128)S(1)} %shard_map.41.in_ref), custom_call_target="tpu_custom_call" | custom-call | tf_op jit(solution)/shard_map/pallas_call | solution.py:247
  206.9 0.0 collective-permute-done
  206.9 0.5 fusion.3
  207.4 9.8 %shard_map.43 = f32[128,512]{1,0:T(8,128)S(1)} custom-call(f32[4,128,512]{2,1,0:T(8,128)S(1)} %bitcast.8), custom_call_target="tpu_custom_call" | custom-call | tf_op jit(solution)/shard_map/pallas_call | solution.py:247
  217.1 0.1 copy.4
  217.2 9.9 %shard_map.44 = f32[64,128]{1,0:T(8,128)S(1)} custom-call(f32[512,128]{1,0:T(8,128)S(1)} %bitcast.9), custom_call_target="tpu_custom_call" | custom-call | tf_op jit(solution)/shard_map/pallas_call | solution.py:177
  227.2 0.6 copy.6
  (1 shorter events, 0.0 us)
Async XLA Ops:
  0.0 55.5 %copy-start.3 = (s32[4]{0:T(128)S(1)}, s32[4]{0:T(128)}, u32[]{:S(2)}) copy-start(s32[4]{0:T(128)} %words_ref.1) | copy-start | bytes 52
  0.0 1.0 copy-start.2
  53.6 1.9 copy-start
  155.7 1.9 copy-start.1
  157.7 49.2 %collective-permute-start = (bf16[512,512]{1,0:T(8,128)(2,1)S(1)}, bf16[512,512]{1,0:T(8,128)(2,1)S(1)}, u32[]{:S(2)}, u32[]{:S(2)}) collective-permute-start(bf16[512,512]{1,0:T(8,128)(2,1)S(1)} %shard_map.39.own_ref), channel_id=1, source_target_pairs={{0,0},{1,8},{2,16},{3,24},{4,1},{5,9},{6,17},{7,25},{8,2},{9,10},{... | collective-permute-start | bytes 1572872 | tf_op jit(solution)/shard_map/ppermute | solution.py:315

commit v5 on v4

--- a/solution.py
+++ b/solution.py
@@ -242,7 +242,8 @@
 
 def fold(scale, stacked, dtype, collective_id):
     par_n, rows, columns = stacked.shape
-    chips, cuts = par_n // 2, 4
+    chips = par_n // 2
+    cuts = 8 if rows * columns >= 1 << 18 else 2
     hold = pltpu.VMEM((chips, rows, columns), jnp.float32)
     return pl.pallas_call(
         functools.partial(fold_kernel, chips, cuts, scale),

time: 228 us -> 228 us (level)
  no operation moved by 1% of the time
where the time goes in v5:
time: 228 us; the launch traced here: 227 us
  Pallas kernels  221 us (97%)
  local copies, waits for them, and re-layouts  5.64 us (2%)
    pallas_call x2, Pallas kernels, gather(): pl.pallas_call(functools.partial(gather_kernel, ex_n), in_specs=[pl.Block...  101 us
    pallas_call x3, Pallas kernels, fold(): pl.pallas_call(functools.partial(fold_kernel, chips, cuts, scale), in_spe...  66.8 us
    pallas_call x1, Pallas kernels, project(): pl.pallas_call(functools.partial(hash_kernel, tile), grid=(amount // dept...  23.9 us
    pallas_call x1, Pallas kernels, precondition(): pl.pallas_call(tiles_kernel, grid=(count,), in_specs=[pl.BlockSpec((1, ro...  18.8 us
    pallas_call x1, Pallas kernels, scatter(): pl.pallas_call(functools.partial(scatter_kernel, ex_n, scale), in_specs=[...  9.47 us
    unnamed x9, local copies, waits for them, and re-layouts  5.52 us
  transfers between devices with their start and end apart: 1, of which 0 were waited for; matrix products, arithmetic and copies ran while one was open for 0% of the time, Pallas kernels for 21%

profile of v5, /device:TPU:0, one launch (start us, length us, event | category | flops | bytes accessed | tf_op | source)
XLA Modules:
  0.0 227.5 jit_solution(9765212060104999458)
XLA Ops:
  0.0 0.0 copy-start.3
  0.0 0.0 copy-start.2
  0.0 1.0 copy-done.2
  1.1 52.5 %shard_map.37 = bf16[8,64,4096]{2,1,0:T(8,128)(2,1)S(1)} custom-call(bf16[64,4096]{1,0:T(8,128)(2,1)S(1)} %copy-done.2), custom_call_target="tpu_custom_call" | custom-call | tf_op jit(solution)/shard_map/pallas_call | solution.py:131
  53.6 0.0 copy-start
  53.6 1.9 copy-done
  55.5 0.0 copy-done.3
  55.5 23.9 %shard_map.38.in_ref = f32[4,512,512]{2,1,0:T(8,128)S(1)} custom-call(s32[4]{0:T(128)S(1)} %copy-done.3, s32[1]{0:T(128)} %bitcast.start_ref, s32[1,2048]{1,0:T(1,128)S(1)} %fusion.cols_ref, bf16[512,4096]{1,0:T(8,128)(2,1)} %bitcast.7), custom_call_target="tpu_custom_call" | custom-call | tf_op jit(solution)/shard_map/pallas_call | solution.py:47
  79.4 27.4 %shard_map.39.own_ref = bf16[512,512]{1,0:T(8,128)(2,1)S(1)} custom-call(f32[4,512,512]{2,1,0:T(8,128)S(1)} %shard_map.38.in_ref), custom_call_target="tpu_custom_call" | custom-call | tf_op jit(solution)/shard_map/pallas_call | solution.py:248
  106.8 49.0 %shard_map.40.feat_ref = bf16[8,512,512]{2,1,0:T(8,128)(2,1)S(1)} custom-call(bf16[512,512]{1,0:T(8,128)(2,1)S(1)} %shard_map.39.own_ref), custom_call_target="tpu_custom_call" | custom-call | tf_op jit(solution)/shard_map/pallas_call | solution.py:131
  155.8 0.0 copy-start.1
  155.8 1.9 copy-done.1
  157.8 0.7 collective-permute-start
  158.5 18.8 %shard_map.41.in_ref = f32[4,512,512]{2,1,0:T(8,128)S(1)} custom-call(bf16[8,512,512]{2,1,0:T(8,128)(2,1)} %copy-done.1, bf16[4096,2048]{1,0:T(8,128)(2,1)} %gram_ref.1), custom_call_target="tpu_custom_call" | custom-call | flops 8589934592 | bytes 25165824 | tf_op jit(solution)/shard_map/pallas_call | solution.py:280
  177.3 29.8 %shard_map.42 = bf16[512,512]{1,0:T(8,128)(2,1)S(1)} custom-call(f32[4,512,512]{2,1,0:T(8,128)S(1)} %shard_map.41.in_ref), custom_call_target="tpu_custom_call" | custom-call | tf_op jit(solution)/shard_map/pallas_call | solution.py:248
  207.1 0.0 collective-permute-done
  207.1 0.5 fusion.3
  207.5 9.7 %shard_map.43 = f32[128,512]{1,0:T(8,128)S(1)} custom-call(f32[4,128,512]{2,1,0:T(8,128)S(1)} %bitcast.8), custom_call_target="tpu_custom_call" | custom-call | tf_op jit(solution)/shard_map/pallas_call | solution.py:248
  217.2 0.1 copy.4
  217.4 9.5 %shard_map.44 = f32[64,128]{1,0:T(8,128)S(1)} custom-call(f32[512,128]{1,0:T(8,128)S(1)} %bitcast.9), custom_call_target="tpu_custom_call" | custom-call | tf_op jit(solution)/shard_map/pallas_call | solution.py:177
  226.8 0.6 copy.6
  (1 shorter events, 0.0 us)
Async XLA Ops:
  0.0 55.5 %copy-start.3 = (s32[4]{0:T(128)S(1)}, s32[4]{0:T(128)}, u32[]{:S(2)}) copy-start(s32[4]{0:T(128)} %words_ref.1) | copy-start | bytes 52
  0.0 1.0 copy-start.2
  53.6 1.9 copy-start
  155.8 1.9 copy-start.1
  157.8 49.3 %collective-permute-start = (bf16[512,512]{1,0:T(8,128)(2,1)S(1)}, bf16[512,512]{1,0:T(8,128)(2,1)S(1)}, u32[]{:S(2)}, u32[]{:S(2)}) collective-permute-start(bf16[512,512]{1,0:T(8,128)(2,1)S(1)} %shard_map.39.own_ref), channel_id=1, source_target_pairs={{0,0},{1,8},{2,16},{3,24},{4,1},{5,9},{6,17},{7,25},{8,2},{9,10},{... | collective-permute-start | bytes 1572872 | tf_op jit(solution)/shard_map/ppermute | solution.py:316
